TPU v7x, 512 devices: a whole 4x8x8 slice. The times are simulated.
512 devices in a mesh: dof: 64 (over z, y_lo, core), real: 8 (over y_hi, x).
Axes of the slice: x: 4, y: 8 (y_hi: 2, y_lo: 4; y = y_hi * 4 + y_lo), z: 8, core: 2. Of those that a mesh axis runs over, the one named last changes fastest.
Arguments:
- mode_panel: bfloat16 [131072, 512], P('dof'), may hold values from -0.31445312 to 0.31445312
- stiff_blocks: bfloat16 [1024, 5, 128, 128], P('dof'), as said below
- stiff_cols: int32 [1024, 5], P('dof'), may hold values from 0 to 1023, as said below
- row_blade: int32 [131072], P('dof'), may hold values from 0 to 3, as said below
- adjusted_values: float32 [512], replicated, may hold values from 4 to 24
- deviations: float32 [128, 4], P('dof'), may hold values from -0.05 to 0.05
- start_block: float32 [512, 128], P('real'), may hold values from -6 to 6
Outputs:
- projected: float32 [4, 512, 512], P(None, 'real')
- subspace: float32 [128, 512, 128], P('dof', 'real')
Inputs may be any that keep to these rules, and one draw needn't show every extreme that they name: `stiff_cols`: each block row's 5 entries are, in some order, the block row itself and the block rows two and one before and one and two after it; where one of those lies outside the grid or in another blade's rows, the block row itself stands in. `stiff_blocks`: the stiffness is symmetric and couples no two blades: the block of block row g at column c is the transpose of the block of block row c at column g, diagonal blocks are symmetric, and stand-in blocks are zero. `row_blade`: block row g belongs to the blade numbered ((g + 8) // 256) mod 4 under a fixed relabelling of the blades; so each blade owns a run of 32768 neighbouring rows, except one blade, which owns the first 31744 rows and the last 1024 rows.
All inputs are finite; a program needn't handle non-finite values.
Results may differ from a plain program's by a relative error of at most 0.003.
Values may be sent and summed in bfloat16 or wider, within the bound.
No kernel may reach another device: no remote copies, remote signals or barrier semaphores. Data moves between devices by JAX's collectives and lax.ppermute only.
A program may use at most 64 MiB of HBM per device.

v0:
```python
import jax
import jax.numpy as jnp
from jax import lax
from jax.sharding import PartitionSpec as P

ADJUSTED_MODES = 512
NBLADE = 4
STEPS = 2
highest_accuracy = lax.Precision.HIGHEST


def with_halo(block, sides, width):
    for axis, dim in sides:
        count = lax.axis_size(axis)
        forward = [(i, i + 1) for i in range(count - 1)]
        backward = [(target, source) for source, target in forward]
        low = lax.ppermute(
            lax.slice_in_dim(block, block.shape[dim] - width, None, axis=dim), axis, forward
        )
        high = lax.ppermute(lax.slice_in_dim(block, 0, width, axis=dim), axis, backward)
        block = jnp.concatenate([low, block, high], axis=dim)
    return block


def multiply_by_blocks(ext_blocks, blocks, columns):
    number = blocks.shape[0]
    size = blocks.shape[2]
    mode_count = ext_blocks.shape[2]
    row_totals = jnp.zeros((number, size, mode_count), jnp.float32)
    for slot_index in range(blocks.shape[1]):
        picked = jnp.take(ext_blocks, columns[:, slot_index], axis=0)
        row_totals = row_totals + jnp.einsum(
            "gab,gbm->gam", blocks[:, slot_index], picked, preferred_element_type=jnp.float32
        )
    return row_totals.reshape(number * size, mode_count).astype(jnp.bfloat16)


def add_projection(portion, offset, mode_panel, row_blade, col_start, owned_rows):
    number = portion.shape[0]
    left_rows = lax.dynamic_slice(mode_panel, (offset, col_start), (number, owned_rows))
    stacked = jnp.concatenate(
        [
            jnp.where((row_blade == blade_index)[:, None], left_rows, jnp.zeros_like(left_rows))
            for blade_index in range(NBLADE)
        ],
        axis=1,
    )
    return lax.dot_general(
        stacked, portion, (((0,), (0,)), ((), ())), preferred_element_type=jnp.float32
    )


def inverse_factor(inner_product_matrix):
    factor = jnp.linalg.cholesky(inner_product_matrix)
    identity = jnp.broadcast_to(
        jnp.eye(inner_product_matrix.shape[-1], dtype=inner_product_matrix.dtype),
        inner_product_matrix.shape,
    )
    return lax.linalg.triangular_solve(factor, identity, left_side=True, lower=True)


def normalize_parts(present_image):
    partial_inner_products = jnp.einsum(
        "eox,eol->exl", present_image, present_image, precision=highest_accuracy
    )
    inner_product_matrix = lax.psum(partial_inner_products, "real") / ADJUSTED_MODES
    inverse = inverse_factor(inner_product_matrix)
    return jnp.einsum("zjs,zts->zjt", present_image, inverse, precision=highest_accuracy)


def on_device(
    mode_panel, stiff_blocks, stiff_cols, row_blade, adjusted_values, deviations, start_block
):
    real_count = lax.axis_size("real")
    owner_index = lax.axis_index("real")
    mode_count = mode_panel.shape[1]
    owned_rows = mode_count // real_count
    block_size = stiff_blocks.shape[2]
    shard_blocks = stiff_blocks.shape[0]
    col_start = owner_index * owned_rows
    extended = with_halo(mode_panel, (("dof", 0),), 2 * block_size)
    ext_blocks = extended.reshape(shard_blocks + 4, block_size, mode_count)
    local_cols = stiff_cols - lax.axis_index("dof") * shard_blocks + 2
    stiff_image = multiply_by_blocks(ext_blocks, stiff_blocks, local_cols)
    blade_parts = add_projection(
        stiff_image, jnp.zeros((), jnp.int32), mode_panel, row_blade, col_start, owned_rows
    )
    summed = lax.psum(blade_parts, "dof")
    projected = summed.reshape(NBLADE, owned_rows, mode_count)
    row_ids = jnp.arange(owned_rows, dtype=jnp.int32) + col_start
    own_values = lax.dynamic_slice_in_dim(adjusted_values, col_start, owned_rows, 0)
    diagonal_part = jnp.where(
        jnp.arange(mode_count, dtype=jnp.int32)[None, :] == row_ids[:, None],
        own_values[:, None],
        jnp.zeros((), jnp.float32),
    )
    realizations = deviations.shape[0]
    subspace_width = start_block.shape[1]
    reduced = (
        jnp.einsum("zb,bjm->zjm", deviations, projected, precision=highest_accuracy)
        + diagonal_part[None]
    )
    current = jnp.broadcast_to(start_block[None], (realizations, owned_rows, subspace_width))
    for iteration in range(STEPS):
        present_image = jnp.einsum(
            "zjk,zks->zjs",
            reduced,
            lax.all_gather(current, "real", axis=1, tiled=True),
            precision=highest_accuracy,
        )
        current = normalize_parts(present_image)
    return (projected, current)


def solution(mesh):
    in_specs = (
        P("dof", None),
        P("dof", None, None, None),
        P("dof", None),
        P("dof"),
        P(),
        P("dof", None),
        P("real", None),
    )
    out_specs = (P(None, "real", None), P("dof", "real", None))
    return jax.shard_map(
        on_device, mesh=mesh, in_specs=in_specs, out_specs=out_specs, check_vma=False
    )
```

profile of v0, /device:TPU:64, one launch (start us, length us, event | category | flops | bytes accessed | tf_op | source)
XLA Modules:
  0.0 967.4 jit_solution(17578840527042316968)
XLA Ops:
  7.2 1.1 fusion.60
  8.3 1.9 collective-permute-start
  10.2 6.3 collective-permute-start.1
  18.0 5.4 broadcast_select_fusion.3
  24.4 2.0 gather_fusion.2
  26.4 2.0 gather_fusion.1
  28.4 2.0 gather_fusion.3
  30.4 2.0 gather_fusion.4
  32.4 2.0 gather_fusion
  34.5 2.7 fusion.3
  42.4 1.6 add_convert_fusion
  44.0 1.3 fusion.15
  45.3 1.1 copy.27
  46.6 44.8 %all_gather.8 = f32[512,128]{1,0:T(8,128)S(1)} all-gather(f32[64,128]{1,0:T(8,128)S(1)} %copy-done.12), channel_id=2, replica_groups=mesh['dof'=64,'real'=8] {'real'}, dimensions={0}, use_global_device_ids=true | all-gather | bytes 294912 | tf_op jit(solution)/shard_map/all_gather | solution.py:108
  91.5 492.6 %all-reduce.4.cloned.1.call-done = f32[4,64,512]{2,0,1:T(4,128)} async-done(((f32[4,64,512]{2,0,1:T(4,128)}), f32[4,64,512]{2,0,1:T(4,128)}) %all-reduce.4.cloned.1.call-update) | async-done | bytes 524304 | tf_op jit(solution)/shard_map/psum | solution.py:88
  584.2 2.1 fusion.14
  586.7 1.0 fusion.61
  588.0 125.4 %all-reduce.6.cloned.1.call-done = f32[2,128,128]{1,2,0:T(8,128)} async-done(((f32[2,128,128]{1,2,0:T(8,128)}), f32[2,128,128]{1,2,0:T(8,128)}) %all-reduce.6.cloned.1.call-update) | async-done | bytes 131088 | tf_op jit(solution)/shard_map/psum | solution.py:66
  715.4 23.5 %custom-call.8 = f32[2,128,128]{2,1,0:T(8,128)S(1)} custom-call(f32[2,128,128]{2,1,0:T(8,128)S(1)} %fusion.48), custom_call_target="Cholesky" | custom-call | tf_op jit(solution)/shard_map/jit(cholesky)/cholesky | solution.py:54
  739.1 19.7 %custom-call.9 = f32[2,1,128,128]{2,3,1,0:T(8,128)S(1)} custom-call(f32[2,1,128,128]{3,2,1,0:T(8,128)S(1)} %select_bitcast_fusion.1), custom_call_target="InvertDiagBlocksLowerTriangular" | custom-call | tf_op jit(solution)/shard_map/triangular_solve/custom-call.0 | solution.py:59
  759.5 45.8 %all_gather.7 = f32[2,512,128]{2,1,0:T(8,128)S(1)} all-gather(f32[2,64,128]{2,1,0:T(8,128)S(1)} %fusion.62), channel_id=1, replica_groups=mesh['dof'=64,'real'=8] {'real'}, dimensions={1}, use_global_device_ids=true | all-gather | bytes 589824 | tf_op jit(solution)/shard_map/all_gather | solution.py:108
  807.8 106.3 %all-reduce.8.cloned.1.call-done = f32[2,128,128]{1,2,0:T(8,128)} async-done(((f32[2,128,128]{1,2,0:T(8,128)}), f32[2,128,128]{1,2,0:T(8,128)}) %all-reduce.8.cloned.1.call-update) | async-done | bytes 131088 | tf_op jit(solution)/shard_map/psum | solution.py:66
  916.0 23.5 %custom-call.10 = f32[2,128,128]{2,1,0:T(8,128)S(1)} custom-call(f32[2,128,128]{2,1,0:T(8,128)S(1)} %fusion.45), custom_call_target="Cholesky" | custom-call | tf_op jit(solution)/shard_map/jit(cholesky)/cholesky | solution.py:54
  939.8 19.7 %custom-call.11 = f32[2,1,128,128]{2,3,1,0:T(8,128)S(1)} custom-call(f32[2,1,128,128]{3,2,1,0:T(8,128)S(1)} %select_bitcast_fusion), custom_call_target="InvertDiagBlocksLowerTriangular" | custom-call | tf_op jit(solution)/shard_map/triangular_solve/custom-call.0 | solution.py:59
  (70 shorter events, 17.5 us)
Async XLA Ops:
  7.2 577.0 %copy-start = (f32[2,4]{1,0:T(2,128)S(1)}, f32[2,4]{1,0:T(2,128)}, u32[]{:S(2)}) copy-start(f32[2,4]{1,0:T(2,128)} %param.17) | copy-start | bytes 100
  7.2 577.0 %all-reduce.4.cloned.1.call-start = ((), (), s32[]{:S(2)}) async-start(), calls=%async_computation | async-start | bytes 1048576 | tf_op jit(solution)/shard_map/psum | solution.py:88
  8.3 15.9 %collective-permute-start = (bf16[256,512]{1,0:T(8,128)(2,1)S(1)}, bf16[256,512]{1,0:T(8,128)(2,1)S(1)}, u32[]{:S(2)}, u32[]{:S(2)}) collective-permute-start(bf16[256,512]{1,0:T(8,128)(2,1)S(1)} %get-tuple-element.23), channel_id=1, source_target_pairs={{0,8},{8,16},{16,24},{24,32},{32,40},{40,48},{48,56},{56,64},{64,7... | collective-permute-start | bytes 786440 | tf_op jit(solution)/shard_map/ppermute | solution.py:17
  10.2 14.0 %collective-permute-start.1 = (bf16[256,512]{1,0:T(8,128)(2,1)S(1)}, bf16[256,512]{1,0:T(8,128)(2,1)S(1)}, u32[]{:S(2)}, u32[]{:S(2)}) collective-permute-start(bf16[256,512]{1,0:T(8,128)(2,1)S(1)} %get-tuple-element.24), channel_id=1, source_target_pairs={{8,0},{16,8},{24,16},{32,24},{40,32},{48,40},{56,48},{64,56},{72,6... | collective-permute-start | bytes 786440 | tf_op jit(solution)/shard_map/ppermute | solution.py:20
  18.0 6.2 copy-start.5
  34.5 2.7 copy-start.3
  34.5 3.2 copy-start.6
  37.6 1.6 copy-start.2
  39.2 1.6 copy-start.4
  40.8 1.6 copy-start.1
  42.4 1.6 copy-start.8
  42.4 1.6 copy-start.9
  42.4 1.6 copy-start.10
  42.4 1.6 copy-start.11
  44.0 2.5 copy-start.12
  46.5 666.9 %all-reduce.6.cloned.1.call-start = ((), (), s32[]{:S(2)}) async-start(), calls=%async_computation.1 | async-start | bytes 262144 | tf_op jit(solution)/shard_map/psum | solution.py:66
  586.7 220.2 %copy-start.7 = (f32[4,64,512]{2,0,1:T(4,128)S(1)}, f32[4,64,512]{2,0,1:T(4,128)}, u32[]{:S(2)}) copy-start(f32[4,64,512]{2,0,1:T(4,128)} %all-reduce.4.cloned.1.call-done) | copy-start | bytes 1572868
  587.8 326.3 %all-reduce.8.cloned.1.call-start = ((), (), s32[]{:S(2)}) async-start(), calls=%async_computation.2 | async-start | bytes 262144 | tf_op jit(solution)/shard_map/psum | solution.py:66
Sparse Core Ops, SparseCore 0:
  46.6 537.4 all-reduce.3
  587.9 125.4 all-reduce.5
  807.0 107.0 all-reduce.7
where the time goes:
time: 968 us; the launch traced here: 967 us
  waiting for transfers between devices  724 us (75%)
  other arithmetic  97.6 us (10%)
  blocking collectives  90.7 us (9%)
  local copies, waits for them, and re-layouts  17.1 us (2%)
  matrix products  15 us (2%)
  between operations  14.1 us (1%)
    psum x1, waiting for transfers between devices, on_device(): summed = lax.psum(blade_parts, 'dof')  493 us
    psum x2, waiting for transfers between devices, normalize_parts(): lax.psum(partial_inner_products, 'real') / ADJUSTED_MODES  232 us
    all_gather x2, blocking collectives, on_device(): lax.all_gather(current, 'real', axis=1, tiled=True)  90.7 us
    another operation x7, other arithmetic, inverse_factor(): factor = jnp.linalg.cholesky(inner_product_matrix)  47.2 us
    another operation x5, other arithmetic, inverse_factor(): lax.linalg.triangular_solve(factor, identity, left_side=True, lower=True)  39.6 us
  transfers between devices with their start and end apart: 5, of which 3 were waited for; matrix products, arithmetic and copies ran while one was open for 1% of the time, Pallas kernels for 0%

commit v1 on v0

--- a/solution.py
+++ b/solution.py
@@ -105,7 +105,9 @@
         present_image = jnp.einsum(
             "zjk,zks->zjs",
             reduced,
-            lax.all_gather(current, "real", axis=1, tiled=True),
+            jnp.concatenate(
+                lax.all_to_all(jnp.stack([current] * lax.axis_size("real")), "real", 0, 0), axis=1
+            ),
             precision=highest_accuracy,
         )
         current = normalize_parts(present_image)

time: 968 us -> 953 us (0.985)
  blocking collectives: 90.7 us -> 17 us
  waiting for transfers between devices: 724 us -> 771 us
    all_gather x2 -> x0, blocking collectives: 90.7 us -> none  [on_device(): lax.all_gather(current, 'real', axis=1, tiled=True)]
    psum x1, waiting for transfers between devices: 493 us -> 537 us  [on_device(): summed = lax.psum(blade_parts, 'dof')]
    all_to_all x0 -> x1, blocking collectives: none -> 17 us  [on_device(): lax.all_to_all(jnp.stack([current] * lax.axis_size('real')), 'real', 0, 0)]
  transfers between devices with their start and end apart: 5 -> 6, of which waited for: 3 -> 3; matrix products, arithmetic and copies ran while one was open for 1% -> 3% of each run, Pallas kernels for 0% -> 0%
where the time goes in v1:
time: 953 us; the launch traced here: 952 us
  waiting for transfers between devices  771 us (81%)
  other arithmetic  97.7 us (10%)
  local copies, waits for them, and re-layouts  18.9 us (2%)
  starting transfers between devices  18.1 us (2%)
  blocking collectives  17 us (2%)
  matrix products  15.1 us (2%)
  between operations  14.1 us (1%)
    psum x1, waiting for transfers between devices, on_device(): summed = lax.psum(blade_parts, 'dof')  537 us
    psum x2, waiting for transfers between devices, normalize_parts(): lax.psum(partial_inner_products, 'real') / ADJUSTED_MODES  234 us
    another operation x7, other arithmetic, inverse_factor(): factor = jnp.linalg.cholesky(inner_product_matrix)  47.2 us
    another operation x5, other arithmetic, inverse_factor(): lax.linalg.triangular_solve(factor, identity, left_side=True, lower=True)  39.6 us
  transfers between devices with their start and end apart: 6, of which 3 were waited for; matrix products, arithmetic and copies ran while one was open for 3% of the time, Pallas kernels for 0%

profile of v1, /device:TPU:64, one launch (start us, length us, event | category | flops | bytes accessed | tf_op | source)
XLA Modules:
  0.0 952.2 jit_solution(187412741088649045)
XLA Ops:
  8.3 1.9 collective-permute-start
  10.2 6.3 collective-permute-start.1
  16.6 1.6 stack.4
  18.2 9.6 %all-to-all-start = ((f32[8,2,64,128]{3,2,1,0:T(8,128)}), f32[8,2,64,128]{3,2,1,0:T(8,128)S(1)}, u32[]{:S(2)}, u32[]{:S(2)}) async-start(f32[8,2,64,128]{3,2,1,0:T(8,128)} %stack.4), calls=%async_computation | async-start | bytes 1048576 | tf_op jit(solution)/shard_map/all_to_all | solution.py:109
  27.9 5.3 broadcast_select_fusion.3
  33.2 1.9 pad_maximum_fusion
  35.0 2.0 gather_fusion.2
  37.0 2.0 gather_fusion.1
  39.1 2.0 gather_fusion.3
  41.1 2.0 gather_fusion.4
  43.1 2.0 gather_fusion
  45.1 2.7 fusion.3
  53.1 1.6 add_convert_fusion
  54.7 1.3 fusion.15
  56.0 1.1 copy.42
  58.1 536.8 %all-reduce.4.cloned.1.call-done = f32[4,64,512]{2,0,1:T(4,128)} async-done(((f32[4,64,512]{2,0,1:T(4,128)}), f32[4,64,512]{2,0,1:T(4,128)}) %all-reduce.4.cloned.1.call-update) | async-done | bytes 524304 | tf_op jit(solution)/shard_map/psum | solution.py:88
  594.8 2.1 fusion.14
  598.8 125.4 %all-reduce.6.cloned.1.call-done = f32[2,128,128]{1,2,0:T(8,128)} async-done(((f32[2,128,128]{1,2,0:T(8,128)}), f32[2,128,128]{1,2,0:T(8,128)}) %all-reduce.6.cloned.1.call-update) | async-done | bytes 131088 | tf_op jit(solution)/shard_map/psum | solution.py:66
  726.1 23.5 %custom-call.8 = f32[2,128,128]{2,1,0:T(8,128)S(1)} custom-call(f32[2,128,128]{2,1,0:T(8,128)S(1)} %fusion.47), custom_call_target="Cholesky" | custom-call | tf_op jit(solution)/shard_map/jit(cholesky)/cholesky | solution.py:54
  749.8 19.7 %custom-call.9 = f32[2,1,128,128]{2,3,1,0:T(8,128)S(1)} custom-call(f32[2,1,128,128]{3,2,1,0:T(8,128)S(1)} %select_bitcast_fusion.1), custom_call_target="InvertDiagBlocksLowerTriangular" | custom-call | tf_op jit(solution)/shard_map/triangular_solve/custom-call.0 | solution.py:59
  770.3 17.0 %all_to_all.10 = f32[8,2,64,128]{3,2,1,0:T(8,128)S(1)} all-to-all(f32[8,2,64,128]{3,2,1,0:T(8,128)S(1)} %stack.5), channel_id=1, replica_groups=mesh['dof'=64,'real'=8] {'real'}, dimensions={0} | all-to-all | bytes 1048576 | tf_op jit(solution)/shard_map/all_to_all | solution.py:109
  789.8 109.1 %all-reduce.8.cloned.1.call-done = f32[2,128,128]{1,2,0:T(8,128)} async-done(((f32[2,128,128]{1,2,0:T(8,128)}), f32[2,128,128]{1,2,0:T(8,128)}) %all-reduce.8.cloned.1.call-update) | async-done | bytes 131088 | tf_op jit(solution)/shard_map/psum | solution.py:66
  900.9 23.5 %custom-call.10 = f32[2,128,128]{2,1,0:T(8,128)S(1)} custom-call(f32[2,128,128]{2,1,0:T(8,128)S(1)} %fusion.44), custom_call_target="Cholesky" | custom-call | tf_op jit(solution)/shard_map/jit(cholesky)/cholesky | solution.py:54
  924.6 19.7 %custom-call.11 = f32[2,1,128,128]{2,3,1,0:T(8,128)S(1)} custom-call(f32[2,1,128,128]{3,2,1,0:T(8,128)S(1)} %select_bitcast_fusion), custom_call_target="InvertDiagBlocksLowerTriangular" | custom-call | tf_op jit(solution)/shard_map/triangular_solve/custom-call.0 | solution.py:59
  (75 shorter events, 18.2 us)
Async XLA Ops:
  7.2 587.7 %copy-start = (f32[2,4]{1,0:T(2,128)S(1)}, f32[2,4]{1,0:T(2,128)}, u32[]{:S(2)}) copy-start(f32[2,4]{1,0:T(2,128)} %param.17) | copy-start | bytes 100
  7.2 20.6 %copy-start.12 = (s32[16,5]{0,1:T(8,128)S(1)}, s32[16,5]{0,1:T(8,128)}, u32[]{:S(2)}) copy-start(s32[16,5]{0,1:T(8,128)} %param.14) | copy-start | bytes 964
  7.2 20.6 %copy-start.11 = (s32[2048]{0:T(1024)S(1)}, s32[2048]{0:T(1024)}, u32[]{:S(2)}) copy-start(s32[2048]{0:T(1024)} %param.15) | copy-start | bytes 24580
  8.3 24.9 %collective-permute-start = (bf16[256,512]{1,0:T(8,128)(2,1)S(1)}, bf16[256,512]{1,0:T(8,128)(2,1)S(1)}, u32[]{:S(2)}, u32[]{:S(2)}) collective-permute-start(bf16[256,512]{1,0:T(8,128)(2,1)S(1)} %get-tuple-element.25), channel_id=1, source_target_pairs={{0,8},{8,16},{16,24},{24,32},{32,40},{40,48},{48,56},{56,64},{64,7... | collective-permute-start | bytes 786440 | tf_op jit(solution)/shard_map/ppermute | solution.py:17
  10.2 23.0 %collective-permute-start.1 = (bf16[256,512]{1,0:T(8,128)(2,1)S(1)}, bf16[256,512]{1,0:T(8,128)(2,1)}, u32[]{:S(2)}, u32[]{:S(2)}) collective-permute-start(bf16[256,512]{1,0:T(8,128)(2,1)S(1)} %get-tuple-element.26), channel_id=1, source_target_pairs={{8,0},{16,8},{24,16},{32,24},{40,32},{48,40},{56,48},{64,56},{72,6... | collective-permute-start | bytes 786440 | tf_op jit(solution)/shard_map/ppermute | solution.py:20
  18.2 578.8 %all-to-all-start = ((f32[8,2,64,128]{3,2,1,0:T(8,128)}), f32[8,2,64,128]{3,2,1,0:T(8,128)S(1)}, u32[]{:S(2)}, u32[]{:S(2)}) async-start(f32[8,2,64,128]{3,2,1,0:T(8,128)} %stack.4), calls=%async_computation | async-start | bytes 1048576 | tf_op jit(solution)/shard_map/all_to_all | solution.py:109
  27.7 567.1 %all-reduce.4.cloned.1.call-start = ((), (), s32[]{:S(2)}) async-start(), calls=%async_computation.2 | async-start | bytes 1048576 | tf_op jit(solution)/shard_map/psum | solution.py:88
  45.1 2.7 copy-start.3
  45.1 3.2 copy-start.5
  48.3 1.6 copy-start.2
  49.9 1.6 copy-start.4
  51.5 1.6 copy-start.1
  53.1 1.6 copy-start.7
  53.1 1.6 copy-start.8
  53.1 1.6 copy-start.9
  53.1 1.6 copy-start.10
  57.1 667.0 %all-reduce.6.cloned.1.call-start = ((), (), s32[]{:S(2)}) async-start(), calls=%async_computation.3 | async-start | bytes 262144 | tf_op jit(solution)/shard_map/psum | solution.py:66
  598.5 300.4 %all-reduce.8.cloned.1.call-start = ((), (), s32[]{:S(2)}) async-start(), calls=%async_computation.4 | async-start | bytes 262144 | tf_op jit(solution)/shard_map/psum | solution.py:66
  769.9 19.0 %copy-start.6 = (f32[4,64,512]{2,0,1:T(4,128)S(1)}, f32[4,64,512]{2,0,1:T(4,128)}, u32[]{:S(2)}) copy-start(f32[4,64,512]{2,0,1:T(4,128)} %all-reduce.4.cloned.1.call-done) | copy-start | bytes 1572868
Sparse Core Ops, SparseCore 0:
  57.3 537.5 all-reduce.3
  598.6 125.4 all-reduce.5
  789.0 109.9 all-reduce.7
